TPU v7x, 512 devices: a whole 4x4x16 slice. The times are simulated.
512 devices in a mesh: basin: 32 (over y, x, core), member: 16 (over z).
Axes of the slice: x: 4, y: 4, z: 16, core: 2. Of those that a mesh axis runs over, the one named last changes fastest.
Arguments:
- initial_reservoir_levels: float32 [64, 4, 32768], P('member', None, 'basin'), may hold values from 0 to 1
- normalized_catchment_settings: float32 [10, 32768], P(None, 'basin'), may hold values from 0 to 1
- rainfall_member_series: float32 [24, 64, 32768], P(None, 'member', 'basin'), may hold values from 0 to 0.03
- surface_heat_celsius: float32 [24, 32768], P(None, 'basin'), may hold values from -12 to 12
- potential_evapotranspiration: float32 [24, 32768], P(None, 'basin'), may hold values from 0 to 0.01
- gauge_measured_values: float32 [128, 32], P('basin'), may hold values from 0 to 1
- gauge_deviation_sigma: float32 [128, 32], P('basin'), may hold values from 0.05 to 0.5
- gauge_perturbation_draws: float32 [128, 32, 64], P('basin', None, 'member'), may hold values from -6 to 6
- gauge_catchment_position: int32 [128, 32], P('basin'), may hold values from 0 to 255
- gauge_present_flag: int32 [128, 32], P('basin'), may hold values 0 or 1
- adjacent_block_list: int32 [128, 3], replicated, may hold values from 0 to 127, as said below
Outputs:
- analysis: float32 [64, 4, 32768], P('member', None, 'basin')
- discharge_series: float32 [24, 64, 32768], P(None, 'member', 'basin')
Inputs may be any that keep to these rules, and one draw needn't show every extreme that they name: `adjacent_block_list`: no block lists itself. Of the 12 entries of any aligned range of 4 blocks, at most 2 point into any one aligned range of 4 blocks, and exactly 2 into some range.
All inputs are finite; a program needn't handle non-finite values. No bound on the sum of `gauge_present_flag` on one device may be relied on, other than what follows from the above.
Results may differ from a plain program's by a relative error of at most 0.0003.
Values sent between devices are 32-bit elements; how exact they have to be, the bound alone decides.
A program may use at most 64 MiB of HBM per device.

v0:
```python
import jax
import jax.numpy as jnp
from jax import lax
from jax.sharding import PartitionSpec as P

NB = 256
OBS = 32
NBR = 3
LOCAL = 128


PARAM_LOW = (-1.5, 0.0002, 0.8, 1.0, 0.4, 0.01, 0.002, 0.0001, 0.1, 0.0001)
PARAM_HIGH = (1.5, 0.002, 4.0, 5.0, 1.0, 0.05, 0.02, 0.002, 0.5, 0.001)


def unpack_params(normalized_catchment_settings):
    return tuple(
        (
            PARAM_LOW[k] + (PARAM_HIGH[k] - PARAM_LOW[k]) * normalized_catchment_settings[k]
            for k in range(10)
        )
    )


def hbv_hour(reservoir_contents, forcing, hydrologic_settings):
    snowpack, moisture, upper_zone, lower_zone = reservoir_contents
    rain_in, air_temp, evap_pot = forcing
    (
        thresh,
        melt_rate,
        field_cap,
        shape_exp,
        evap_limit,
        quick_rate,
        upper_rate,
        lower_rate,
        upper_limit,
        percolation,
    ) = hydrologic_settings
    snow_share = jnp.clip((thresh + 1.0 - air_temp) * 0.5, 0.0, 1.0)
    snowpack = snowpack + snow_share * rain_in
    snowmelt = jnp.minimum(melt_rate * jnp.maximum(air_temp - thresh, 0.0), snowpack)
    snowpack = snowpack - snowmelt
    inflow = (1.0 - snow_share) * rain_in + snowmelt
    recharge = inflow * jnp.power(moisture / field_cap, shape_exp)
    moisture = moisture + inflow - recharge
    excess = jnp.maximum(moisture - field_cap, 0.0)
    moisture = moisture - excess
    actual = jnp.minimum(evap_pot * jnp.minimum(moisture / (evap_limit * field_cap), 1.0), moisture)
    moisture = moisture - actual
    upper_zone = upper_zone + recharge + excess
    perc_flow = jnp.minimum(percolation, upper_zone)
    upper_zone = upper_zone - perc_flow
    lower_zone = lower_zone + perc_flow
    quick_flow = quick_rate * jnp.maximum(upper_zone - upper_limit, 0.0)
    slow_flow = upper_rate * upper_zone
    base_flow = lower_rate * lower_zone
    upper_zone = upper_zone - quick_flow - slow_flow
    lower_zone = lower_zone - base_flow
    return ((snowpack, moisture, upper_zone, lower_zone), quick_flow + slow_flow + base_flow)


def predict_ensemble_discharge(
    initial_reservoir_levels,
    normalized_catchment_settings,
    rainfall_member_series,
    surface_heat_celsius,
    potential_evapotranspiration,
):
    hydrologic_settings = unpack_params(normalized_catchment_settings)
    reservoir_contents = (
        initial_reservoir_levels[:, 0],
        initial_reservoir_levels[:, 1],
        initial_reservoir_levels[:, 2],
        initial_reservoir_levels[:, 3],
    )

    def advance_single_interval(carry, forcing):
        new_state, runoff = hbv_hour(carry, forcing, hydrologic_settings)
        return (new_state, 100.0 * runoff)

    reservoir_contents, discharge_series = lax.scan(
        advance_single_interval,
        reservoir_contents,
        (rainfall_member_series, surface_heat_celsius, potential_evapotranspiration),
    )
    return (reservoir_contents, discharge_series, hydrologic_settings)


def solve_blocks(matrix, rhs):
    factor = jnp.linalg.cholesky(matrix)
    return jax.vmap(lambda lower_tri, right: jax.scipy.linalg.cho_solve((lower_tri, True), right))(
        factor, rhs
    )


def noise_term(scales):
    return scales[:, :, None] ** 2 * jnp.eye(LOCAL, dtype=jnp.float32)


def centred_terms(state_rows, local_pred, local_pert, local_avail, state_sum, pred_sum, members):
    state_anom = state_rows - state_sum / members
    anomaly = local_avail * (local_pred - pred_sum / members)
    innovation = jnp.transpose(local_avail * (local_pert - local_pred), (1, 2, 0))
    return (state_anom, anomaly, innovation)


def on_device(
    initial_reservoir_levels,
    normalized_catchment_settings,
    rainfall_member_series,
    surface_heat_celsius,
    potential_evapotranspiration,
    gauge_measured_values,
    gauge_deviation_sigma,
    gauge_perturbation_draws,
    gauge_catchment_position,
    gauge_present_flag,
    adjacent_block_list,
):
    highest = lax.Precision.HIGHEST
    reservoir_contents, discharge_series, hydrologic_settings = predict_ensemble_discharge(
        initial_reservoir_levels,
        normalized_catchment_settings,
        rainfall_member_series,
        surface_heat_celsius,
        potential_evapotranspiration,
    )
    snowpack, moisture, upper_zone, lower_zone = reservoir_contents
    local_members = moisture.shape[0]
    blk_count = gauge_measured_values.shape[0]
    members = local_members * lax.axis_size("member")
    wetness = 0.45 * moisture / hydrologic_settings[2]
    onehot = (gauge_catchment_position[..., None] == jnp.arange(NB, dtype=jnp.int32)).astype(
        jnp.float32
    )
    gauge_side = jnp.einsum(
        "bon,mbn->mbo",
        onehot,
        discharge_series[-1].reshape(local_members, blk_count, NB),
        precision=highest,
    )
    smap_side = jnp.einsum(
        "bon,mbn->mbo", onehot, wetness.reshape(local_members, blk_count, NB), precision=highest
    )
    slot_gauge = jnp.arange(OBS) < OBS // 2
    predicted = jnp.where(slot_gauge, gauge_side, smap_side)
    perturbed = gauge_measured_values[None] + gauge_deviation_sigma[None] * jnp.transpose(
        gauge_perturbation_draws, (2, 0, 1)
    )
    avail = gauge_present_flag.astype(jnp.float32)
    pred_pack = jnp.transpose(predicted, (1, 0, 2)).reshape(blk_count, local_members * OBS)
    pert_pack = jnp.transpose(perturbed, (1, 0, 2)).reshape(blk_count, local_members * OBS)
    entries = blk_count * NBR
    own_index = lax.axis_index("basin")
    own_list = lax.dynamic_slice_in_dim(
        adjacent_block_list, own_index * blk_count, blk_count, 0
    ).reshape(entries)
    gathered = (
        lax.all_gather(pred_pack, "basin", axis=0, tiled=True),
        lax.all_gather(pert_pack, "basin", axis=0, tiled=True),
        lax.all_gather(gauge_deviation_sigma, "basin", axis=0, tiled=True),
        lax.all_gather(avail, "basin", axis=0, tiled=True),
    )
    far_data = tuple((jnp.take(piece, own_list, axis=0) for piece in gathered))
    far_pred, far_pert, far_sd, far_avail = far_data

    def spread_members(piece):
        shaped = piece.reshape(blk_count, NBR, local_members, OBS)
        return jnp.transpose(shaped, (2, 0, 1, 3)).reshape(local_members, blk_count, NBR * OBS)

    local_pred = jnp.concatenate([predicted, spread_members(far_pred)], axis=2)
    local_pert = jnp.concatenate([perturbed, spread_members(far_pert)], axis=2)
    local_sd = jnp.concatenate(
        [gauge_deviation_sigma, far_sd.reshape(blk_count, NBR * OBS)], axis=1
    )
    local_avail = jnp.concatenate([avail, far_avail.reshape(blk_count, NBR * OBS)], axis=1)
    state_rows = jnp.concatenate(
        [
            moisture.reshape(local_members, blk_count, NB),
            upper_zone.reshape(local_members, blk_count, NB),
        ],
        axis=2,
    )
    scale = 1.0 / (members - 1)
    state_sum, pred_sum = lax.psum(
        (jnp.sum(state_rows, axis=0), jnp.sum(local_pred, axis=0)), "member"
    )
    state_anom, anomaly, innovation = centred_terms(
        state_rows, local_pred, local_pert, local_avail, state_sum, pred_sum, members
    )
    cov_part = jnp.einsum("mbl,mbk->blk", anomaly, anomaly, precision=highest)
    cross_part = jnp.einsum("mbr,mbl->brl", state_anom, anomaly, precision=highest)
    cov_sum, cross_sum = lax.psum((cov_part, cross_part), "member")
    weights = solve_blocks(cov_sum * scale + noise_term(local_sd), innovation)
    increment = jnp.einsum("brl,blm->mbr", cross_sum * scale, weights, precision=highest)
    updated = state_rows + increment
    moisture_new = updated[..., :NB].reshape(local_members, -1)
    upper_new = updated[..., NB:].reshape(local_members, -1)
    analysis = jnp.stack([snowpack, moisture_new, upper_new, lower_zone], axis=1)
    return (analysis, discharge_series)


def solution(mesh):
    placed = (
        P("member", None, "basin"),
        P(None, "basin"),
        P(None, "member", "basin"),
        P(None, "basin"),
        P(None, "basin"),
        P("basin", None),
        P("basin", None),
        P("basin", None, "member"),
        P("basin", None),
        P("basin", None),
        P(),
    )
    return jax.shard_map(
        on_device,
        mesh=mesh,
        in_specs=placed,
        out_specs=(P("member", None, "basin"), P(None, "member", "basin")),
        check_vma=False,
    )
```

profile of v0, /device:TPU:2, one launch (start us, length us, event | category | flops | bytes accessed | tf_op | source)
XLA Modules:
  0.0 499.2 jit_solution(2323201928278323684)
XLA Ops:
  8.1 1.1 multiply_add_fusion.2
  9.3 91.8 %while.20 = (s32[]{:T(128)}, f32[4,1024]{1,0:T(4,128)S(1)}, f32[4,1024]{1,0:T(4,128)S(1)}, f32[4,1024]{1,0:T(4,128)S(1)}, f32[4,1024]{1,0:T(4,128)S(1)}, /*index...) while((s32[]{:T(128)}, f32[4,1024]{1,0:T(4,128)S(1)}, ...), condition=%wide.region_1.2_spmd, body=%wide.region_0.1_spmd.sunk | while | flops 225282 | bytes 385729 | solution.py:82
  10.1 1.4 fusion.40
  12.3 0.8 minimum_subtract_fusion.4
  14.0 1.4 fusion.40
  16.2 0.8 minimum_subtract_fusion.4
  17.8 1.4 fusion.40
  20.0 0.8 minimum_subtract_fusion.4
  21.6 1.4 fusion.40
  23.8 0.8 minimum_subtract_fusion.4
  25.4 1.4 fusion.40
  27.6 0.8 minimum_subtract_fusion.4
  29.3 1.4 fusion.40
  31.5 0.8 minimum_subtract_fusion.4
  33.1 1.4 fusion.40
  35.3 0.8 minimum_subtract_fusion.4
  36.9 1.4 fusion.40
  40.7 1.4 fusion.40
  44.6 1.4 fusion.40
  48.4 1.4 fusion.40
  52.2 1.4 fusion.40
  56.0 1.4 fusion.40
  59.9 1.4 fusion.40
  63.7 1.4 fusion.40
  67.5 1.4 fusion.40
  71.3 1.4 fusion.40
  75.2 1.4 fusion.40
  77.3 0.8 minimum_subtract_fusion.4
  79.0 1.4 fusion.40
  82.8 1.4 fusion.40
  85.0 0.8 minimum_subtract_fusion.4
  86.6 1.4 fusion.40
  90.4 1.4 fusion.40
  92.6 0.8 minimum_subtract_fusion.4
  94.3 1.4 fusion.40
  98.1 1.4 fusion.40
  102.5 27.2 %all-gather.1 = f32[32,4,128]{2,1,0:T(4,128)S(1)} all-gather(f32[1,4,128]{2,1,0:T(4,128)S(1)} %reshape.213), channel_id=1, replica_groups=mesh['basin'=32,'member'=16] {'basin'}, dimensions={0}, use_global_device_ids=true | all-gather | bytes 67584 | tf_op jit(solution)/shard_map/all_gather | solution.py:160
  130.4 21.5 %all-gather.3 = f32[32,4,128]{2,1,0:T(4,128)S(1)} all-gather(f32[1,4,128]{2,1,0:T(4,128)S(1)} %reshape.217), channel_id=1, replica_groups=mesh['basin'=32,'member'=16] {'basin'}, dimensions={0}, use_global_device_ids=true | all-gather | bytes 67584 | tf_op jit(solution)/shard_map/all_gather | solution.py:161
  153.5 60.3 %all-reduce = (f32[4,128]{1,0:T(4,128)S(1)}, f32[4,512]{1,0:T(4,128)S(1)}) all-reduce(f32[4,128]{1,0:T(4,128)S(1)} %fusion.31, f32[4,512]{1,0:T(4,128)S(1)} %fusion.19), channel_id=1, replica_groups=mesh['basin'=32,'member'=16] {'member'}, use_global_device_ids=true, to_apply=%region_3.6 | all-reduce | flops 2560 | bytes 20480 | tf_op jit(solution)/shard_map/psum | solution.py:186
  214.5 23.0 %all-gather = f32[32,4,32]{2,1,0:T(4,128)S(1)} all-gather(f32[1,4,32]{2,1,0:T(4,128)S(1)} %get-tuple-element.311), channel_id=1, replica_groups=mesh['basin'=32,'member'=16] {'basin'}, dimensions={0}, use_global_device_ids=true | all-gather | bytes 16896 | tf_op jit(solution)/shard_map/all_gather | solution.py:163
  238.1 22.8 %all-gather.2 = f32[32,4,32]{2,1,0:T(4,128)S(1)} all-gather(f32[1,4,32]{2,1,0:T(4,128)S(1)} %bitcast.145), channel_id=1, replica_groups=mesh['basin'=32,'member'=16] {'basin'}, dimensions={0}, use_global_device_ids=true | all-gather | bytes 16896 | tf_op jit(solution)/shard_map/all_gather | solution.py:162
  261.7 1.3 fusion.25
  263.0 2.8 fusion.15
  266.2 135.2 %all-reduce.4.cloned.1.call-done = (f32[4,128,128]{1,2,0:T(8,128)}, f32[4,512,128]{2,1,0:T(8,128)}) async-done(((f32[4,128,128]{1,2,0:T(8,128)}, f32[4,512,128]{2,1,0:T(8,128)}), (f32[4,128,128]{1,2,0:T(8,128)}, f32[4,512,128]{2,1,0:T(8,128)})) %all-reduce.4.cloned.1.call-update) | async-done | bytes 1310736 | tf_op jit(solution)/shard_map/psum | solution.py:194
  401.4 1.0 multiply_add_fusion.1
  403.3 46.9 %custom-call.11 = f32[4,128,128]{2,1,0:T(8,128)S(1)} custom-call(f32[4,128,128]{2,1,0:T(8,128)S(1)} %fusion.11), custom_call_target="Cholesky" | custom-call | tf_op jit(solution)/shard_map/jit(cholesky)/cholesky | solution.py:91
  450.5 39.3 %custom-call.12 = f32[4,1,128,128]{2,3,1,0:T(8,128)S(1)} custom-call(f32[4,1,128,128]{3,2,1,0:T(8,128)S(1)} %select_bitcast_fusion), custom_call_target="InvertDiagBlocksLowerTriangular" | custom-call | tf_op jit(solution)/shard_map/vmap(jit(_cho_solve))/triangular_solve | solution.py:92
  490.7 0.9 fusion.4
  (138 shorter events, 58.6 us)
Async XLA Ops:
  7.2 0.7 copy-start
  7.2 2.1 copy-start.3
  7.2 394.2 %all-reduce.4.cloned.1.call-start = ((), (), s32[]{:S(2)}) async-start(), calls=%async_computation | async-start | bytes 2621440 | tf_op jit(solution)/shard_map/psum | solution.py:194
  101.2 0.7 copy-start.8
  102.5 27.2 %copy-start.5 = (f32[4,32,4]{1,2,0:T(4,128)S(1)}, f32[4,32,4]{1,2,0:T(4,128)}, u32[]{:S(2)}) copy-start(f32[4,32,4]{1,2,0:T(4,128)} %param.24) | copy-start | bytes 6148
  129.6 0.7 copy-start.4
  129.6 0.7 copy-start.6
  213.9 0.7 copy-start.7
  402.3 1.0 copy-start.2
  403.3 87.4 %copy-start.1 = (f32[4,512,128]{2,1,0:T(8,128)S(1)}, f32[4,512,128]{2,1,0:T(8,128)}, u32[]{:S(2)}) copy-start(f32[4,512,128]{2,1,0:T(8,128)} %get-tuple-element.278) | copy-start | bytes 3145732
Sparse Core Ops, SparseCore 0:
  266.0 135.3 all-reduce.3
where the time goes:
time: 506 us; the launch traced here: 499 us
  other arithmetic  162 us (32%)
  blocking collectives  155 us (31%)
  waiting for transfers between devices  135 us (27%)
  local copies, waits for them, and re-layouts  25.9 us (5%)
  between operations  14.3 us (3%)
  matrix products  6.38 us (1%)
    psum x1, waiting for transfers between devices, on_device(): cov_sum, cross_sum = lax.psum((cov_part, cross_part), 'member')  135 us
    psum x1, blocking collectives, on_device(): lax.psum((jnp.sum(state_rows, axis=0), jnp.sum(local_pred, axis=0)), 'mem...  60.3 us
    another operation x4, other arithmetic, solve_blocks(): factor = jnp.linalg.cholesky(matrix)  47.1 us
    another operation x3, other arithmetic, solve_blocks(): jax.scipy.linalg.cho_solve((lower_tri, True), right)  39.4 us
    dynamic_update_slice x24, other arithmetic, predict_ensemble_discharge(): lax.scan(advance_single_interval, reservoir_contents, (rainfall_member_se...  34.3 us
    all_gather x1, blocking collectives, on_device(): lax.all_gather(pred_pack, 'basin', axis=0, tiled=True)  27.2 us
    all_gather x1, blocking collectives, on_device(): lax.all_gather(avail, 'basin', axis=0, tiled=True)  23 us
    all_gather x1, blocking collectives, on_device(): lax.all_gather(gauge_deviation_sigma, 'basin', axis=0, tiled=True)  22.8 us
  transfers between devices with their start and end apart: 1, of which 1 were waited for; matrix products, arithmetic and copies ran while one was open for 0% of the time, Pallas kernels for 0%

commit v1 on v0

v1 whole, which is shorter than its diff:
```python
import functools
import math

import jax
import jax.numpy as jnp
from jax import lax
from jax.experimental import pallas as pl
from jax.experimental.pallas import tpu as pltpu
from jax.sharding import PartitionSpec as P

f32 = jnp.float32
NB = 256
OBS = 32
NBR = 3
BLK = 4
HOURS = 24
MEM = 4
NBAS = 32
NMEM = 16
MESH = pl.DeviceIdType.MESH
HIGHEST = lax.Precision.HIGHEST
NT = (((1,), (1,)), ((), ()))
LOG2E = math.log2(math.e)

PARAM_LOW = (-1.5, 0.0002, 0.8, 1.0, 0.4, 0.01, 0.002, 0.0001, 0.1, 0.0001)
PARAM_HIGH = (1.5, 0.002, 4.0, 5.0, 1.0, 0.05, 0.02, 0.002, 0.5, 0.001)


def hour_step(states, rains, temp, evap, par):
    (thresh, melt_rate, field_cap, inv_cap, shape_log, inv_limit,
     quick_rate, upper_rate, lower_rate, upper_limit, percolation) = par
    share = jnp.clip((thresh + 1.0 - temp) * 0.5, 0.0, 1.0)
    dry = 1.0 - share
    melt_cap = melt_rate * jnp.maximum(temp - thresh, 0.0)
    out = []
    flows = []
    for (snow, moist, upper, lower), rain in zip(states, rains):
        snow = snow + share * rain
        melt = jnp.minimum(melt_cap, snow)
        snow = snow - melt
        inflow = dry * rain + melt
        recharge = inflow * jnp.exp2(shape_log * jnp.log(moist * inv_cap))
        moist = moist + inflow - recharge
        excess = jnp.maximum(moist - field_cap, 0.0)
        moist = moist - excess
        actual = jnp.minimum(evap * jnp.minimum(moist * inv_limit, 1.0), moist)
        moist = moist - actual
        upper = upper + recharge + excess
        perc = jnp.minimum(percolation, upper)
        upper = upper - perc
        lower = lower + perc
        quick = quick_rate * jnp.maximum(upper - upper_limit, 0.0)
        slow = upper_rate * upper
        base = lower_rate * lower
        upper = upper - quick - slow
        lower = lower - base
        out.append((snow, moist, upper, lower))
        flows.append(100.0 * (quick + slow + base))
    return out, flows


def eliminate(blocks):
    blocks = [list(b) for b in blocks]
    shape = (8, 128)
    for k in range(0, 64, 2):
        kt, kr = divmod(k, 8)
        for b in blocks:
            r0 = jnp.broadcast_to(b[kt][kr:kr + 1, :], shape)
            r1 = jnp.broadcast_to(b[kt][kr + 1:kr + 2, :], shape)
            a = jnp.broadcast_to(r0[:, k:k + 1], shape)
            o = jnp.broadcast_to(r0[:, k + 1:k + 2], shape)
            d = jnp.broadcast_to(r1[:, k + 1:k + 2], shape)
            inv = 1.0 / (a * d - o * o)
            n0 = (d * r0 - o * r1) * inv
            n1 = (a * r1 - o * r0) * inv
            for t in range(kt, 9):
                c0 = jnp.broadcast_to(b[t][:, k:k + 1], shape)
                c1 = jnp.broadcast_to(b[t][:, k + 1:k + 2], shape)
                b[t] = b[t] - (c0 * n0 + c1 * n1)
    return [b[8] for b in blocks]


def kernel(init, prm, rain, temp, evap, meas, sig, draws, pos, flag, adj, an_out, q_out,
           init_v, prm_v, rain_v, temp_v, evap_v, meas_v, sig_v, draws_v, pos_v, flag_v,
           prow_v, q_v, an_v, oh_v, turn_v, gath, sz, xz,
           in_sem, out_sem, gs_sem, gr_sem, ss_sem, sr_sem, xs_sem, xr_sem):
    me_b = lax.axis_index("basin")
    me_z = lax.axis_index("member")
    shape = (8, 128)
    lane = lax.broadcasted_iota(jnp.int32, shape, 1)
    row = lax.broadcasted_iota(jnp.int32, shape, 0)
    top = row < 4

    def zmod(v):
        return lax.rem(v + 2 * NMEM, NMEM)

    barrier = pltpu.get_barrier_semaphore()

    def greet(d, carry):
        pl.semaphore_signal(barrier, inc=1, device_id={"basin": lax.rem(me_b + d, NBAS)}, device_id_type=MESH)
        return carry

    lax.fori_loop(1, NBAS, greet, 0)
    for d in (1, -1, 2, -2, 3, -3, 4, -4):
        pl.semaphore_signal(barrier, inc=1, device_id={"member": zmod(me_z + d)}, device_id_type=MESH)

    loads = []
    for src, dst in ((sig, sig_v), (flag, flag_v), (meas, meas_v), (draws, draws_v), (pos, pos_v),
                     (prm, prm_v), (temp, temp_v), (evap, evap_v), (init, init_v), (rain, rain_v)):
        cp = pltpu.make_async_copy(src, dst, in_sem.at[len(loads)])
        cp.start()
        loads.append(cp)
    for cp in loads[:5]:
        cp.wait()

    weights, perts, places = [], [], []
    for i in range(BLK):
        sd = sig_v[i:i + 1, :]
        weights.append(jnp.broadcast_to(flag_v[i:i + 1, :].astype(f32) / sd, (8, OBS)))
        pert = meas_v[i:i + 1, :] + sd * draws_v[i]
        perts.append(jnp.concatenate([pert, pert], axis=0))
        places.append(jnp.broadcast_to(pos_v[i:i + 1, :] + NB * i, (8, OBS)))
    weight = jnp.concatenate(weights, axis=1)
    pert = jnp.concatenate(perts, axis=1)
    place = jnp.concatenate(places, axis=1)
    place16 = jnp.concatenate([place, place], axis=0)
    row16 = lax.broadcasted_iota(jnp.int32, (16, 128), 0)
    for j in range(64):
        oh_v[16 * j:16 * j + 16, :] = jnp.where(place16 == row16 + 16 * j, 1.0, 0.0).astype(jnp.bfloat16)

    loads[5].wait()
    par = []
    for s in range(8):
        prow_v[8 * s:8 * s + 8, :] = prm_v[0:8, 128 * s:128 * s + 128]
        prow_v[64 + 2 * s:66 + 2 * s, :] = prm_v[8:10, 128 * s:128 * s + 128]
    for k in range(10):
        v = prow_v[pl.ds(k, 8, stride=8), :] if k < 8 else prow_v[pl.ds(64 + k - 8, 8, stride=2), :]
        par.append(PARAM_LOW[k] + (PARAM_HIGH[k] - PARAM_LOW[k]) * v)
    tt, cfmax, fc, beta, lp, k0, k1, k2, uzl, perc = par
    inv_fc = 1.0 / fc
    hydro = (tt, cfmax, fc, inv_fc, beta * LOG2E, 1.0 / (lp * fc), k0, k1, k2, uzl, perc)

    for cp in loads[6:]:
        cp.wait()
    states = [tuple(init_v[pl.ds(32 * m + c, 8, stride=4), :] for c in range(4)) for m in range(MEM)]

    def eight_hours(chunk, states):
        flows = None
        for h in range(8):
            base = chunk * 256 + 32 * h
            rains = [rain_v[pl.ds(base + m, 8, stride=4), :] for m in range(MEM)]
            tmp = temp_v[pl.ds(chunk * 64 + h, 8, stride=8), :]
            eva = evap_v[pl.ds(chunk * 64 + h, 8, stride=8), :]
            states, flows = hour_step(states, rains, tmp, eva, hydro)
            for m in range(MEM):
                q_v[pl.ds(base + m, 8, stride=4), :] = flows[m]
        return states, flows

    states, flows = lax.fori_loop(
        0, 3, lambda c, s: eight_hours(c, s[0]),
        (states, [jnp.zeros(shape, f32)] * MEM))
    q_copy = pltpu.make_async_copy(q_v, q_out, out_sem.at[0])
    q_copy.start()

    for m in range(MEM):
        turn_v[8 * m:8 * m + 8, :] = states[m][1]
        turn_v[32 + 8 * m:40 + 8 * m, :] = states[m][2]
    for s in range(8):
        xz[0, 8 * s:8 * s + 8, :] = turn_v[pl.ds(s, 8, stride=8), :]
    for m in range(MEM):
        turn_v[64 + 8 * m:72 + 8 * m, :] = flows[m]
        turn_v[96 + 8 * m:104 + 8 * m, :] = 0.45 * states[m][1] * inv_fc
    field = jnp.concatenate([turn_v[pl.ds(64 + s, 8, stride=8), :] for s in range(8)], axis=1)
    hi = field.astype(jnp.bfloat16).astype(f32)
    mid = (field - hi).astype(jnp.bfloat16).astype(f32)
    low = field - hi - mid
    stack = jnp.concatenate([hi, mid, low, jnp.zeros_like(low)], axis=0).astype(jnp.bfloat16)
    picked = jnp.dot(stack, oh_v[...], preferred_element_type=f32)
    both = picked[0:8] + picked[8:16] + picked[16:24]
    swapped = pltpu.roll(both, 4, 0)
    pred = jnp.where(top == (lax.rem(lane, OBS) < OBS // 2), both, swapped)
    tile = weight * jnp.where(top, pred, pert - pred)
    gath[31] = tile

    pl.semaphore_wait(barrier, NBAS - 1 + 8)

    def x_copy(slot):
        if slot <= 8:
            src, to = slot - 1, 1
        else:
            src, to = (slot + 1) % NMEM, -1
        return pltpu.make_async_remote_copy(
            xz.at[src], xz.at[slot], xs_sem.at[slot - 1], xr_sem.at[slot - 1],
            device_id={"member": zmod(me_z + to)}, device_id_type=MESH)

    def g_copy(d):
        return pltpu.make_async_remote_copy(
            gath.at[31], gath.at[d - 1], gs_sem.at[d - 1], gr_sem.at[d - 1],
            device_id={"basin": lax.rem(me_b + d, NBAS)}, device_id_type=MESH)

    def s_copy(src, slot, to):
        return pltpu.make_async_remote_copy(
            sz.at[src], sz.at[slot], ss_sem.at[slot - 1], sr_sem.at[slot - 1],
            device_id={"member": zmod(me_z + to)}, device_id_type=MESH)

    def g_start(d, carry):
        g_copy(d).start()
        return carry

    lax.fori_loop(1, NBAS, g_start, 0)
    x_copy(1).start()
    x_copy(15).start()

    def x_next(step):
        x_copy(step).wait_recv()
        x_copy(step + 1).start()
        if step < 7:
            x_copy(16 - step).wait_recv()
            x_copy(15 - step).start()

    x_next(1)
    x_next(2)

    def g_wait(d, carry):
        g_copy(d).wait_recv()
        return carry

    lax.fori_loop(1, NBAS, g_wait, 0)

    local = []
    for i in range(BLK):
        piece = tile if i == 0 else pltpu.roll(tile, 128 - OBS * i, 1)
        for j in range(NBR):
            n = adj[j, me_b * BLK + i]
            slot = lax.rem(me_b + 2 * NBAS - 1 - lax.div(n, BLK), NBAS)
            shift = lax.rem(OBS * (j + 1) + 128 - OBS * lax.rem(n, BLK), 128)
            far = pltpu.roll(gath[slot], shift, 1)
            piece = jnp.where(lax.div(lane, OBS) == j + 1, far, piece)
        local.append(piece)
    turned = [pltpu.roll(p, 4, 0) for p in local]
    for p in range(2):
        sz[0, 8 * p:8 * p + 8, :] = jnp.where(top, local[2 * p], turned[2 * p + 1])
    obs_side = [jnp.where(top, t, p) for t, p in zip(turned, local)]

    for d in (4, 3, 2, 1):
        s_copy(0, d, d).start()
        s_copy(0, NMEM - d, -d).start()

    x_next(3)
    x_next(4)
    s_copy(0, 4, 4).wait_recv()
    for d in (4, 3, 2, 1):
        s_copy(4, 4 + d, d).start()
    s_copy(0, 12, -4).wait_recv()
    for d in (3, 2, 1):
        s_copy(12, 12 - d, -d).start()
    x_next(5)
    x_next(6)
    x_next(7)
    for slot in (1, 2, 3, 13, 14, 15):
        s_copy(0, slot, 1).wait_recv()
    for slot in (5, 6, 7, 8, 9, 10, 11):
        s_copy(0, slot, 1).wait_recv()

    systems = []
    big_row = lax.broadcasted_iota(jnp.int32, (72, 128), 0)
    big_lane = lax.broadcasted_iota(jnp.int32, (72, 128), 1)
    unit = jnp.where((big_row < 64) & ((big_lane == big_row) | (big_lane == big_row + 64)), 1.0, 0.0)
    for i in range(BLK):
        p, odd = divmod(i, 2)
        tiles = []
        for q in range(8):
            a = sz[q, 8 * p:8 * p + 8, :]
            b = sz[q + 8, 8 * p:8 * p + 8, :]
            if odd:
                tiles.append(jnp.where(top, pltpu.roll(a, 4, 0), b))
            else:
                tiles.append(jnp.where(top, a, pltpu.roll(b, 4, 0)))
        total = functools.reduce(jnp.add, tiles)
        mean = jnp.sum(total, axis=0, keepdims=True) * (1.0 / 64.0)
        centred = jnp.concatenate(tiles, axis=0) - mean
        left = jnp.concatenate([centred, obs_side[i]], axis=0)
        right = jnp.concatenate([centred, jnp.zeros_like(centred)], axis=0)
        gram = lax.dot_general(left, right, NT, precision=HIGHEST, preferred_element_type=f32)
        system = gram * (1.0 / 63.0) + unit
        systems.append([system[8 * t:8 * t + 8] for t in range(9)])
    solved = eliminate(systems)

    x_copy(8).wait_recv()
    x_copy(9).wait_recv()

    keep = top == (lax.rem(lane, 8) < 4)
    for i in range(BLK):
        t = jnp.where(lane >= 64, -solved[i], 0.0)
        t = t - jnp.sum(t, axis=1, keepdims=True) * (1.0 / 64.0)
        coef = jnp.where(
            lane >= 64,
            jnp.where(top, pltpu.roll(t, 124, 1), t),
            jnp.where(top, pltpu.roll(t, 64, 1), pltpu.roll(t, 68, 1)))
        coef = jnp.where(keep, coef, 0.0)
        for s in (2 * i, 2 * i + 1):
            stored = xz[:, 8 * s:8 * s + 8, :].reshape(128, 128)
            new = xz[0, 8 * s:8 * s + 8, :] + jnp.dot(
                coef, stored, precision=HIGHEST, preferred_element_type=f32)
            an_v[pl.ds(4 * s + 1, 4, stride=32), :] = new[0:4]
            an_v[pl.ds(4 * s + 2, 4, stride=32), :] = new[4:8]
    for m in range(MEM):
        an_v[pl.ds(32 * m, 8, stride=4), :] = states[m][0]
        an_v[pl.ds(32 * m + 3, 8, stride=4), :] = states[m][3]
    an_copy = pltpu.make_async_copy(an_v, an_out, out_sem.at[1])
    an_copy.start()

    def g_done(d, carry):
        g_copy(d).wait_send()
        return carry

    lax.fori_loop(1, NBAS, g_done, 0)
    for slot in range(1, NMEM):
        s_copy(0, slot, 1).wait_send()
        x_copy(slot).wait_send()
    q_copy.wait()
    an_copy.wait()


def on_device(init, prm, rain, temp, evap, meas, sig, draws, pos, flag, adj):
    def member_rows(a):
        return a.reshape(-1, 4, 8, 128).transpose(0, 2, 1, 3).reshape(-1, 128)

    def hour_rows(a):
        return a.reshape(3, 8, 8, 128).transpose(0, 2, 1, 3).reshape(192, 128)

    any_spec = pl.BlockSpec(memory_space=pl.ANY)
    dma = pltpu.SemaphoreType.DMA
    an, q = pl.pallas_call(
        kernel,
        out_shape=(jax.ShapeDtypeStruct((128, 128), f32), jax.ShapeDtypeStruct((768, 128), f32)),
        in_specs=[any_spec] * 10 + [pl.BlockSpec(memory_space=pltpu.SMEM)],
        out_specs=(any_spec, any_spec),
        scratch_shapes=[
            pltpu.VMEM((128, 128), f32), pltpu.VMEM((10, 1024), f32), pltpu.VMEM((768, 128), f32),
            pltpu.VMEM((192, 128), f32), pltpu.VMEM((192, 128), f32),
            pltpu.VMEM((4, 32), f32), pltpu.VMEM((4, 32), f32), pltpu.VMEM((4, 4, 32), f32),
            pltpu.VMEM((4, 32), jnp.int32), pltpu.VMEM((4, 32), jnp.int32),
            pltpu.VMEM((80, 128), f32), pltpu.VMEM((768, 128), f32), pltpu.VMEM((128, 128), f32),
            pltpu.VMEM((1024, 128), jnp.bfloat16), pltpu.VMEM((128, 128), f32),
            pltpu.VMEM((32, 8, 128), f32), pltpu.VMEM((16, 16, 128), f32), pltpu.VMEM((16, 64, 128), f32),
            dma((10,)), dma((2,)), dma((31,)), dma((31,)), dma((15,)), dma((15,)), dma((15,)), dma((15,)),
        ],
        compiler_params=pltpu.CompilerParams(collective_id=0, has_side_effects=True),
    )(member_rows(init), prm, member_rows(rain), hour_rows(temp), hour_rows(evap), meas, sig,
      draws.transpose(0, 2, 1), pos, flag, adj.T)

    def whole(a):
        return a.reshape(-1, 8, 4, 128).transpose(0, 2, 1, 3).reshape(-1, 4, 1024)

    return whole(an), whole(q)


def solution(mesh):
    placed = (
        P("member", None, "basin"),
        P(None, "basin"),
        P(None, "member", "basin"),
        P(None, "basin"),
        P(None, "basin"),
        P("basin", None),
        P("basin", None),
        P("basin", None, "member"),
        P("basin", None),
        P("basin", None),
        P(),
    )
    return jax.shard_map(
        on_device,
        mesh=mesh,
        in_specs=placed,
        out_specs=(P("member", None, "basin"), P(None, "member", "basin")),
        check_vma=False,
    )
```

time: 506 us -> 49.7 us (0.10)
  the two profiles are of different devices: /device:TPU:2 before, /device:TPU:32 now
where the time goes in v1:
time: 49.7 us; the launch traced here: 49.4 us
  Pallas kernels  45.6 us (92%)
  local copies, waits for them, and re-layouts  3.24 us (7%)
  between operations  0.64 us (1%)
    pallas_call x1, Pallas kernels, on_device(): pl.pallas_call(kernel, out_shape=(jax.ShapeDtypeStruct((128, 128), f32),...  45.6 us
    unnamed x2, local copies, waits for them, and re-layouts  3.24 us

profile of v1, /device:TPU:32, one launch (start us, length us, event | category | flops | bytes accessed | tf_op | source)
XLA Modules:
  0.0 49.4 jit_solution(13157463774054418190)
XLA Ops:
  0.6 45.6 %shard_map.122 = (f32[128,128]{1,0:T(8,128)}, f32[768,128]{1,0:T(8,128)}) custom-call(f32[128,128]{1,0:T(8,128)} %bitcast.36, f32[10,1024]{1,0:T(8,128)} %prm.1, f32[768,128]{1,0:T(8,128)} %bitcast.32, f32[192,128]{1,0:T(8,128)} %bitcast.34, f32[192,128]{1,0:T(8,128)} %bitcast.35, f32[4,32]{1,0:T(4,128)} %meas.1, f32[4,32]{1,0:T(4,128)} %sig.1, ...), custom_call_target="tpu_custom_call" | custom-call | tf_op jit(solution)/shard_map/pallas_call | solution.py:334
  46.2 1.5 %copy.19 = f32[4,4,1024]{2,1,0:T(4,128)} copy(f32[4,4,1024]{2,1,0:T(4,128)} %bitcast.37) | data formatting | bytes 131072
  47.7 1.8 %copy.20 = f32[24,4,1024]{2,1,0:T(4,128)} copy(f32[24,4,1024]{2,1,0:T(4,128)} %bitcast.33) | data formatting | bytes 786432

commit v2 on v1

--- a/solution.py
+++ b/solution.py
@@ -17,6 +17,12 @@
 MEM = 4
 NBAS = 32
 NMEM = 16
+X_REACH = 3
+S_REACH = 4
+REACH = 4
+XLATE = 1
+LIMIT = 16 * 1024 * 1024
+
 MESH = pl.DeviceIdType.MESH
 HIGHEST = lax.Precision.HIGHEST
 NT = (((1,), (1,)), ((), ()))
@@ -62,28 +68,42 @@
 def eliminate(blocks):
     blocks = [list(b) for b in blocks]
     shape = (8, 128)
-    for k in range(0, 64, 2):
+
+    def wide(v, k):
+        return jnp.broadcast_to(v[:, k:k + 1], shape)
+
+    for k in range(0, 64, 4):
         kt, kr = divmod(k, 8)
         for b in blocks:
-            r0 = jnp.broadcast_to(b[kt][kr:kr + 1, :], shape)
-            r1 = jnp.broadcast_to(b[kt][kr + 1:kr + 2, :], shape)
-            a = jnp.broadcast_to(r0[:, k:k + 1], shape)
-            o = jnp.broadcast_to(r0[:, k + 1:k + 2], shape)
-            d = jnp.broadcast_to(r1[:, k + 1:k + 2], shape)
-            inv = 1.0 / (a * d - o * o)
-            n0 = (d * r0 - o * r1) * inv
-            n1 = (a * r1 - o * r0) * inv
-            for t in range(kt, 9):
-                c0 = jnp.broadcast_to(b[t][:, k:k + 1], shape)
-                c1 = jnp.broadcast_to(b[t][:, k + 1:k + 2], shape)
-                b[t] = b[t] - (c0 * n0 + c1 * n1)
+            r = [jnp.broadcast_to(b[kt][kr + j:kr + j + 1, :], shape) for j in range(4)]
+            a00, a01, b00, b01 = (wide(r[0], k + j) for j in range(4))
+            a11, b10, b11 = (wide(r[1], k + j) for j in (1, 2, 3))
+            d00, d01 = (wide(r[2], k + j) for j in (2, 3))
+            d11 = wide(r[3], k + 3)
+            inv = 1.0 / (a00 * a11 - a01 * a01)
+            i00, i01, i11 = a11 * inv, -a01 * inv, a00 * inv
+            g00, g01 = i00 * b00 + i01 * b10, i00 * b01 + i01 * b11
+            g10, g11 = i01 * b00 + i11 * b10, i01 * b01 + i11 * b11
+            s00 = d00 - (b00 * g00 + b10 * g10)
+            s01 = d01 - (b00 * g01 + b10 * g11)
+            s11 = d11 - (b01 * g01 + b11 * g11)
+            jnv = 1.0 / (s00 * s11 - s01 * s01)
+            q2 = r[2] - (g00 * r[0] + g10 * r[1])
+            q3 = r[3] - (g01 * r[0] + g11 * r[1])
+            n2 = (s11 * q2 - s01 * q3) * jnv
+            n3 = (s00 * q3 - s01 * q2) * jnv
+            n0 = i00 * r[0] + i01 * r[1] - (g00 * n2 + g01 * n3)
+            n1 = i01 * r[0] + i11 * r[1] - (g10 * n2 + g11 * n3)
+            for t in range(kt + kr // 4, 9):
+                c = [wide(b[t], k + j) for j in range(4)]
+                b[t] = b[t] - ((c[0] * n0 + c[1] * n1) + (c[2] * n2 + c[3] * n3))
     return [b[8] for b in blocks]
 
 
-def kernel(init, prm, rain, temp, evap, meas, sig, draws, pos, flag, adj, an_out, q_out,
-           init_v, prm_v, rain_v, temp_v, evap_v, meas_v, sig_v, draws_v, pos_v, flag_v,
-           prow_v, q_v, an_v, oh_v, turn_v, gath, sz, xz,
-           in_sem, out_sem, gs_sem, gr_sem, ss_sem, sr_sem, xs_sem, xr_sem):
+def kernel(init, prm, rain, temp, evap, meas, sig, draws, pos, flag, adj_hbm, an_v, q_v,
+           init_v, prm_v, rain_v, temp_v, evap_v, meas_v, sig_v, draws_v, pos_v, flag_v, adj,
+           prow_v, oh_v, turn_v, gath, sz, xz,
+           in_sem, gs_sem, gr_sem, ss_sem, sr_sem, xs_sem, xr_sem):
     me_b = lax.axis_index("basin")
     me_z = lax.axis_index("member")
     shape = (8, 128)
@@ -101,12 +121,13 @@
         return carry
 
     lax.fori_loop(1, NBAS, greet, 0)
-    for d in (1, -1, 2, -2, 3, -3, 4, -4):
-        pl.semaphore_signal(barrier, inc=1, device_id={"member": zmod(me_z + d)}, device_id_type=MESH)
+    for d in range(1, REACH + 1):
+        for to in {d, NMEM - d}:
+            pl.semaphore_signal(barrier, inc=1, device_id={"member": zmod(me_z + to)}, device_id_type=MESH)
 
     loads = []
     for src, dst in ((sig, sig_v), (flag, flag_v), (meas, meas_v), (draws, draws_v), (pos, pos_v),
-                     (prm, prm_v), (temp, temp_v), (evap, evap_v), (init, init_v), (rain, rain_v)):
+                     (prm, prm_v), (temp, temp_v), (evap, evap_v), (init, init_v), (rain, rain_v), (adj_hbm, adj)):
         cp = pltpu.make_async_copy(src, dst, in_sem.at[len(loads)])
         cp.start()
         loads.append(cp)
@@ -159,8 +180,6 @@
     states, flows = lax.fori_loop(
         0, 3, lambda c, s: eight_hours(c, s[0]),
         (states, [jnp.zeros(shape, f32)] * MEM))
-    q_copy = pltpu.make_async_copy(q_v, q_out, out_sem.at[0])
-    q_copy.start()
 
     for m in range(MEM):
         turn_v[8 * m:8 * m + 8, :] = states[m][1]
@@ -182,50 +201,44 @@
     tile = weight * jnp.where(top, pred, pert - pred)
     gath[31] = tile
 
-    pl.semaphore_wait(barrier, NBAS - 1 + 8)
-
-    def x_copy(slot):
-        if slot <= 8:
-            src, to = slot - 1, 1
-        else:
-            src, to = (slot + 1) % NMEM, -1
+    pl.semaphore_wait(barrier, NBAS - 1 + min(2 * REACH, NMEM - 1))
+
+    def z_copy(buf, send, recv, src, slot, to):
         return pltpu.make_async_remote_copy(
-            xz.at[src], xz.at[slot], xs_sem.at[slot - 1], xr_sem.at[slot - 1],
+            buf.at[src], buf.at[slot], send.at[slot - 1], recv.at[slot - 1],
             device_id={"member": zmod(me_z + to)}, device_id_type=MESH)
+
+    def x_copy(src, slot, to):
+        return z_copy(xz, xs_sem, xr_sem, src, slot, to)
+
+    def s_copy(src, slot, to):
+        return z_copy(sz, ss_sem, sr_sem, src, slot, to)
+
+    def spread(copy, reach, base):
+        if base:
+            copy(0, base, 1).wait_recv()
+            copy(0, NMEM - base, 1).wait_recv()
+        for d in range(min(reach, 8 - base), 0, -1):
+            copy(base, base + d, d).start()
+            if base + d < 8:
+                copy((NMEM - base) % NMEM, NMEM - base - d, -d).start()
+
+    def settle(copy, reach):
+        for slot in range(1, NMEM):
+            hop = min(slot, NMEM - slot)
+            if hop % reach or hop == 8:
+                copy(0, slot, 1).wait_recv()
 
     def g_copy(d):
         return pltpu.make_async_remote_copy(
             gath.at[31], gath.at[d - 1], gs_sem.at[d - 1], gr_sem.at[d - 1],
             device_id={"basin": lax.rem(me_b + d, NBAS)}, device_id_type=MESH)
 
-    def s_copy(src, slot, to):
-        return pltpu.make_async_remote_copy(
-            sz.at[src], sz.at[slot], ss_sem.at[slot - 1], sr_sem.at[slot - 1],
-            device_id={"member": zmod(me_z + to)}, device_id_type=MESH)
-
-    def g_start(d, carry):
+    for d in range(1, NBAS):
         g_copy(d).start()
-        return carry
-
-    lax.fori_loop(1, NBAS, g_start, 0)
-    x_copy(1).start()
-    x_copy(15).start()
-
-    def x_next(step):
-        x_copy(step).wait_recv()
-        x_copy(step + 1).start()
-        if step < 7:
-            x_copy(16 - step).wait_recv()
-            x_copy(15 - step).start()
-
-    x_next(1)
-    x_next(2)
-
-    def g_wait(d, carry):
+    spread(x_copy, X_REACH, 0)
+    for d in range(1, NBAS):
         g_copy(d).wait_recv()
-        return carry
-
-    lax.fori_loop(1, NBAS, g_wait, 0)
 
     local = []
     for i in range(BLK):
@@ -242,25 +255,15 @@
         sz[0, 8 * p:8 * p + 8, :] = jnp.where(top, local[2 * p], turned[2 * p + 1])
     obs_side = [jnp.where(top, t, p) for t, p in zip(turned, local)]
 
-    for d in (4, 3, 2, 1):
-        s_copy(0, d, d).start()
-        s_copy(0, NMEM - d, -d).start()
-
-    x_next(3)
-    x_next(4)
-    s_copy(0, 4, 4).wait_recv()
-    for d in (4, 3, 2, 1):
-        s_copy(4, 4 + d, d).start()
-    s_copy(0, 12, -4).wait_recv()
-    for d in (3, 2, 1):
-        s_copy(12, 12 - d, -d).start()
-    x_next(5)
-    x_next(6)
-    x_next(7)
-    for slot in (1, 2, 3, 13, 14, 15):
-        s_copy(0, slot, 1).wait_recv()
-    for slot in (5, 6, 7, 8, 9, 10, 11):
-        s_copy(0, slot, 1).wait_recv()
+    spread(s_copy, S_REACH, 0)
+    bases = list(range(X_REACH, 8, X_REACH))
+    for base in bases[:len(bases) - XLATE]:
+        spread(x_copy, X_REACH, base)
+    for base in range(S_REACH, 8, S_REACH):
+        spread(s_copy, S_REACH, base)
+    settle(s_copy, S_REACH)
+    for base in bases[len(bases) - XLATE:]:
+        spread(x_copy, X_REACH, base)
 
     systems = []
     big_row = lax.broadcasted_iota(jnp.int32, (72, 128), 0)
@@ -286,8 +289,7 @@
         systems.append([system[8 * t:8 * t + 8] for t in range(9)])
     solved = eliminate(systems)
 
-    x_copy(8).wait_recv()
-    x_copy(9).wait_recv()
+    settle(x_copy, X_REACH)
 
     keep = top == (lax.rem(lane, 8) < 4)
     for i in range(BLK):
@@ -307,19 +309,20 @@
     for m in range(MEM):
         an_v[pl.ds(32 * m, 8, stride=4), :] = states[m][0]
         an_v[pl.ds(32 * m + 3, 8, stride=4), :] = states[m][3]
-    an_copy = pltpu.make_async_copy(an_v, an_out, out_sem.at[1])
-    an_copy.start()
-
-    def g_done(d, carry):
+
+    for d in range(1, NBAS):
         g_copy(d).wait_send()
-        return carry
-
-    lax.fori_loop(1, NBAS, g_done, 0)
     for slot in range(1, NMEM):
         s_copy(0, slot, 1).wait_send()
-        x_copy(slot).wait_send()
-    q_copy.wait()
-    an_copy.wait()
+        x_copy(0, slot, 1).wait_send()
+
+
+def hand_over(an, q, an_out, q_out, sem):
+    copies = [pltpu.make_async_copy(q, q_out, sem.at[0]), pltpu.make_async_copy(an, an_out, sem.at[1])]
+    for cp in copies:
+        cp.start()
+    for cp in copies:
+        cp.wait()
 
 
 def on_device(init, prm, rain, temp, evap, meas, sig, draws, pos, flag, adj):
@@ -330,25 +333,36 @@
         return a.reshape(3, 8, 8, 128).transpose(0, 2, 1, 3).reshape(192, 128)
 
     any_spec = pl.BlockSpec(memory_space=pl.ANY)
+    hbm_spec = pl.BlockSpec(memory_space=pltpu.HBM)
     dma = pltpu.SemaphoreType.DMA
     an, q = pl.pallas_call(
         kernel,
         out_shape=(jax.ShapeDtypeStruct((128, 128), f32), jax.ShapeDtypeStruct((768, 128), f32)),
-        in_specs=[any_spec] * 10 + [pl.BlockSpec(memory_space=pltpu.SMEM)],
-        out_specs=(any_spec, any_spec),
+        in_specs=[hbm_spec] * 11,
+        out_specs=(pl.BlockSpec(memory_space=pltpu.VMEM),) * 2,
         scratch_shapes=[
             pltpu.VMEM((128, 128), f32), pltpu.VMEM((10, 1024), f32), pltpu.VMEM((768, 128), f32),
             pltpu.VMEM((192, 128), f32), pltpu.VMEM((192, 128), f32),
             pltpu.VMEM((4, 32), f32), pltpu.VMEM((4, 32), f32), pltpu.VMEM((4, 4, 32), f32),
-            pltpu.VMEM((4, 32), jnp.int32), pltpu.VMEM((4, 32), jnp.int32),
-            pltpu.VMEM((80, 128), f32), pltpu.VMEM((768, 128), f32), pltpu.VMEM((128, 128), f32),
+            pltpu.VMEM((4, 32), jnp.int32), pltpu.VMEM((4, 32), jnp.int32), pltpu.SMEM((3, 128), jnp.int32),
+            pltpu.VMEM((80, 128), f32),
             pltpu.VMEM((1024, 128), jnp.bfloat16), pltpu.VMEM((128, 128), f32),
             pltpu.VMEM((32, 8, 128), f32), pltpu.VMEM((16, 16, 128), f32), pltpu.VMEM((16, 64, 128), f32),
-            dma((10,)), dma((2,)), dma((31,)), dma((31,)), dma((15,)), dma((15,)), dma((15,)), dma((15,)),
+            dma((11,)), dma((31,)), dma((31,)), dma((15,)), dma((15,)), dma((15,)), dma((15,)),
         ],
-        compiler_params=pltpu.CompilerParams(collective_id=0, has_side_effects=True),
-    )(member_rows(init), prm, member_rows(rain), hour_rows(temp), hour_rows(evap), meas, sig,
-      draws.transpose(0, 2, 1), pos, flag, adj.T)
+        compiler_params=pltpu.CompilerParams(collective_id=0, has_side_effects=True, vmem_limit_bytes=LIMIT),
+    )(*[pltpu.with_memory_space_constraint(a, pltpu.HBM) for a in (
+        member_rows(init), prm, member_rows(rain), hour_rows(temp), hour_rows(evap), meas, sig,
+        draws.transpose(0, 2, 1), pos, flag, adj.T)])
+
+    an, q = pl.pallas_call(
+        hand_over,
+        out_shape=(jax.ShapeDtypeStruct((128, 128), f32), jax.ShapeDtypeStruct((768, 128), f32)),
+        in_specs=[any_spec] * 2,
+        out_specs=(any_spec, any_spec),
+        scratch_shapes=[dma((2,))],
+        compiler_params=pltpu.CompilerParams(vmem_limit_bytes=LIMIT),
+    )(an, q)
 
     def whole(a):
         return a.reshape(-1, 8, 4, 128).transpose(0, 2, 1, 3).reshape(-1, 4, 1024)

time: 49.7 us -> 38.2 us (0.77)
  the two profiles are of different devices: /device:TPU:32 before, /device:TPU:1 now
where the time goes in v2:
time: 38.2 us; the launch traced here: 38 us
  Pallas kernels  37.4 us (98%)
  between operations  0.64 us (2%)
    pallas_call x1, Pallas kernels, on_device(): pl.pallas_call(kernel, out_shape=(jax.ShapeDtypeStruct((128, 128), f32),...  36.6 us
    pallas_call x1, Pallas kernels, on_device(): pl.pallas_call(hand_over, out_shape=(jax.ShapeDtypeStruct((128, 128), f32...  0.78 us

profile of v2, /device:TPU:1, one launch (start us, length us, event | category | flops | bytes accessed | tf_op | source)
XLA Modules:
  0.0 38.0 jit_solution(15647592973803088828)
XLA Ops:
  0.6 36.6 %shard_map.122 = (f32[128,128]{1,0:T(8,128)S(1)}, f32[768,128]{1,0:T(8,128)S(1)}) custom-call(f32[128,128]{1,0:T(8,128)} %bitcast.35, f32[10,1024]{1,0:T(8,128)} %prm.1, f32[768,128]{1,0:T(8,128)} %bitcast.32, f32[192,128]{1,0:T(8,128)} %bitcast.33, f32[192,128]{1,0:T(8,128)} %bitcast.34, f32[4,32]{1,0:T(4,128)} %meas.1, f32[4,32]{1,0:T(4,128)} %sig.1, ...), custom_call_target="tpu_custom_call" | custom-call | tf_op jit(solution)/shard_map/pallas_call | solution.py:338
  37.2 0.8 %shard_map.123 = (f32[128,128]{1,0:T(8,128)}, f32[768,128]{1,0:T(8,128)}) custom-call(f32[128,128]{1,0:T(8,128)S(1)} %get-tuple-element.6.an, f32[768,128]{1,0:T(8,128)S(1)} %get-tuple-element.7.q), custom_call_target="tpu_custom_call" | custom-call | tf_op jit(solution)/shard_map/pallas_call | solution.py:358

commit v3 on v2

--- a/solution.py
+++ b/solution.py
@@ -20,7 +20,7 @@
 X_REACH = 3
 S_REACH = 4
 REACH = 4
-XLATE = 1
+ORDER = ('S0', 'X3', 'S4', 'W', 'X6')
 LIMIT = 16 * 1024 * 1024
 
 MESH = pl.DeviceIdType.MESH
@@ -30,6 +30,10 @@
 
 PARAM_LOW = (-1.5, 0.0002, 0.8, 1.0, 0.4, 0.01, 0.002, 0.0001, 0.1, 0.0001)
 PARAM_HIGH = (1.5, 0.002, 4.0, 5.0, 1.0, 0.05, 0.02, 0.002, 0.5, 0.001)
+
+
+STEPS = sorted(((dy, dx, dc) for dy in range(4) for dx in range(4) for dc in range(2)),
+               key=lambda o: (-min(o[0], 4 - o[0]) - min(o[1], 4 - o[1]), -o[2]))[:-1]
 
 
 def hour_step(states, rains, temp, evap, par):
@@ -65,21 +69,32 @@
     return out, flows
 
 
-def eliminate(blocks):
-    blocks = [list(b) for b in blocks]
+def eliminate(pairs):
+    pairs = [list(b) for b in pairs]
     shape = (8, 128)
-
-    def wide(v, k):
-        return jnp.broadcast_to(v[:, k:k + 1], shape)
+    lane = lax.broadcasted_iota(jnp.int32, shape, 1)
+    half = lane - lane % 64
+
+    def take(v, index, axis):
+        return jnp.take_along_axis(v, index, axis=axis, mode="promise_in_bounds")
 
     for k in range(0, 64, 4):
         kt, kr = divmod(k, 8)
-        for b in blocks:
+        here = [lane % 64 == k + j for j in range(4)]
+        inside = (lane % 64 >= k) & (lane % 64 < k + 4)
+        columns = [half + (k + j) for j in range(4)]
+        for b in pairs:
+            head = [take(b[kt], columns[j], 1) for j in range(4)]
+
+            def at(i, j):
+                return jnp.broadcast_to(head[j][kr + i:kr + i + 1, :], shape)
+
             r = [jnp.broadcast_to(b[kt][kr + j:kr + j + 1, :], shape) for j in range(4)]
-            a00, a01, b00, b01 = (wide(r[0], k + j) for j in range(4))
-            a11, b10, b11 = (wide(r[1], k + j) for j in (1, 2, 3))
-            d00, d01 = (wide(r[2], k + j) for j in (2, 3))
-            d11 = wide(r[3], k + 3)
+            r = [jnp.where(inside, jnp.where(here[j], 1.0, 0.0), r[j]) for j in range(4)]
+            a00, a01, b00, b01 = (at(0, j) for j in range(4))
+            a11, b10, b11 = (at(1, j) for j in (1, 2, 3))
+            d00, d01 = (at(2, j) for j in (2, 3))
+            d11 = at(3, 3)
             inv = 1.0 / (a00 * a11 - a01 * a01)
             i00, i01, i11 = a11 * inv, -a01 * inv, a00 * inv
             g00, g01 = i00 * b00 + i01 * b10, i00 * b01 + i01 * b11
@@ -95,9 +110,9 @@
             n0 = i00 * r[0] + i01 * r[1] - (g00 * n2 + g01 * n3)
             n1 = i01 * r[0] + i11 * r[1] - (g10 * n2 + g11 * n3)
             for t in range(kt + kr // 4, 9):
-                c = [wide(b[t], k + j) for j in range(4)]
-                b[t] = b[t] - ((c[0] * n0 + c[1] * n1) + (c[2] * n2 + c[3] * n3))
-    return [b[8] for b in blocks]
+                c = head if t == kt else [take(b[t], columns[j], 1) for j in range(4)]
+                b[t] = jnp.where(inside, 0.0, b[t]) - ((c[0] * n0 + c[1] * n1) + (c[2] * n2 + c[3] * n3))
+    return [b[8] for b in pairs]
 
 
 def kernel(init, prm, rain, temp, evap, meas, sig, draws, pos, flag, adj_hbm, an_v, q_v,
@@ -114,23 +129,27 @@
     def zmod(v):
         return lax.rem(v + 2 * NMEM, NMEM)
 
-    barrier = pltpu.get_barrier_semaphore()
-
-    def greet(d, carry):
-        pl.semaphore_signal(barrier, inc=1, device_id={"basin": lax.rem(me_b + d, NBAS)}, device_id_type=MESH)
-        return carry
-
-    lax.fori_loop(1, NBAS, greet, 0)
-    for d in range(1, REACH + 1):
-        for to in {d, NMEM - d}:
-            pl.semaphore_signal(barrier, inc=1, device_id={"member": zmod(me_z + to)}, device_id_type=MESH)
-
     loads = []
     for src, dst in ((sig, sig_v), (flag, flag_v), (meas, meas_v), (draws, draws_v), (pos, pos_v),
                      (prm, prm_v), (temp, temp_v), (evap, evap_v), (init, init_v), (rain, rain_v), (adj_hbm, adj)):
         cp = pltpu.make_async_copy(src, dst, in_sem.at[len(loads)])
         cp.start()
         loads.append(cp)
+
+    barrier = pltpu.get_barrier_semaphore()
+
+    me_y, me_x, me_c = me_b // 8, (me_b // 2) % 4, me_b % 2
+
+    def there(step):
+        dy, dx, dc = step
+        return {"basin": ((me_y + dy) % 4 * 4 + (me_x + dx) % 4) * 2 + (me_c + dc) % 2}
+
+    for step in STEPS:
+        pl.semaphore_signal(barrier, inc=1, device_id=there(step), device_id_type=MESH)
+    for d in range(1, REACH + 1):
+        for to in {d, NMEM - d}:
+            pl.semaphore_signal(barrier, inc=1, device_id={"member": zmod(me_z + to)}, device_id_type=MESH)
+
     for cp in loads[:5]:
         cp.wait()
 
@@ -199,7 +218,7 @@
     swapped = pltpu.roll(both, 4, 0)
     pred = jnp.where(top == (lax.rem(lane, OBS) < OBS // 2), both, swapped)
     tile = weight * jnp.where(top, pred, pert - pred)
-    gath[31] = tile
+    gath[0] = tile
 
     pl.semaphore_wait(barrier, NBAS - 1 + min(2 * REACH, NMEM - 1))
 
@@ -229,23 +248,24 @@
             if hop % reach or hop == 8:
                 copy(0, slot, 1).wait_recv()
 
-    def g_copy(d):
+    def g_copy(step):
+        slot = (step[0] * 4 + step[1]) * 2 + step[2]
         return pltpu.make_async_remote_copy(
-            gath.at[31], gath.at[d - 1], gs_sem.at[d - 1], gr_sem.at[d - 1],
-            device_id={"basin": lax.rem(me_b + d, NBAS)}, device_id_type=MESH)
-
-    for d in range(1, NBAS):
-        g_copy(d).start()
+            gath.at[0], gath.at[slot], gs_sem.at[slot - 1], gr_sem.at[slot - 1],
+            device_id=there(step), device_id_type=MESH)
+
+    for step in STEPS:
+        g_copy(step).start()
     spread(x_copy, X_REACH, 0)
-    for d in range(1, NBAS):
-        g_copy(d).wait_recv()
+    for step in reversed(STEPS):
+        g_copy(step).wait_recv()
 
     local = []
     for i in range(BLK):
         piece = tile if i == 0 else pltpu.roll(tile, 128 - OBS * i, 1)
         for j in range(NBR):
             n = adj[j, me_b * BLK + i]
-            slot = lax.rem(me_b + 2 * NBAS - 1 - lax.div(n, BLK), NBAS)
+            slot = ((me_y + 4 - n // 32) % 4 * 4 + (me_x + 4 - n // 8 % 4) % 4) * 2 + (me_c + 2 - n // 4 % 2) % 2
             shift = lax.rem(OBS * (j + 1) + 128 - OBS * lax.rem(n, BLK), 128)
             far = pltpu.roll(gath[slot], shift, 1)
             piece = jnp.where(lax.div(lane, OBS) == j + 1, far, piece)
@@ -255,35 +275,38 @@
         sz[0, 8 * p:8 * p + 8, :] = jnp.where(top, local[2 * p], turned[2 * p + 1])
     obs_side = [jnp.where(top, t, p) for t, p in zip(turned, local)]
 
-    spread(s_copy, S_REACH, 0)
-    bases = list(range(X_REACH, 8, X_REACH))
-    for base in bases[:len(bases) - XLATE]:
-        spread(x_copy, X_REACH, base)
-    for base in range(S_REACH, 8, S_REACH):
-        spread(s_copy, S_REACH, base)
-    settle(s_copy, S_REACH)
-    for base in bases[len(bases) - XLATE:]:
-        spread(x_copy, X_REACH, base)
+    for what in ORDER:
+        if what == "W":
+            settle(s_copy, S_REACH)
+        else:
+            copy, reach = (s_copy, S_REACH) if what[0] == "S" else (x_copy, X_REACH)
+            spread(copy, reach, int(what[1:]))
 
     systems = []
     big_row = lax.broadcasted_iota(jnp.int32, (72, 128), 0)
     big_lane = lax.broadcasted_iota(jnp.int32, (72, 128), 1)
-    unit = jnp.where((big_row < 64) & ((big_lane == big_row) | (big_lane == big_row + 64)), 1.0, 0.0)
-    for i in range(BLK):
-        p, odd = divmod(i, 2)
-        tiles = []
-        for q in range(8):
-            a = sz[q, 8 * p:8 * p + 8, :]
-            b = sz[q + 8, 8 * p:8 * p + 8, :]
-            if odd:
-                tiles.append(jnp.where(top, pltpu.roll(a, 4, 0), b))
-            else:
-                tiles.append(jnp.where(top, a, pltpu.roll(b, 4, 0)))
-        total = functools.reduce(jnp.add, tiles)
-        mean = jnp.sum(total, axis=0, keepdims=True) * (1.0 / 64.0)
-        centred = jnp.concatenate(tiles, axis=0) - mean
-        left = jnp.concatenate([centred, obs_side[i]], axis=0)
-        right = jnp.concatenate([centred, jnp.zeros_like(centred)], axis=0)
+    unit = jnp.where((big_row < 64) & (big_lane % 64 == big_row), 1.0, 0.0)
+    for p in range(2):
+        lefts, centres = [], []
+        for odd in range(2):
+            tiles = []
+            for q in range(8):
+                a = sz[q, 8 * p:8 * p + 8, :]
+                b = sz[q + 8, 8 * p:8 * p + 8, :]
+                if odd:
+                    tiles.append(jnp.where(top, pltpu.roll(a, 4, 0), b))
+                else:
+                    tiles.append(jnp.where(top, a, pltpu.roll(b, 4, 0)))
+            total = functools.reduce(jnp.add, tiles)
+            mean = jnp.sum(total, axis=0, keepdims=True) * (1.0 / 64.0)
+            centred = jnp.concatenate(tiles, axis=0) - mean
+            centres.append(centred)
+            lefts.append(jnp.concatenate([centred, obs_side[2 * p + odd]], axis=0))
+        none = jnp.zeros_like(centres[0])
+        left = jnp.concatenate(lefts, axis=1)
+        right = jnp.concatenate([
+            jnp.concatenate([centres[0], none], axis=1),
+            jnp.concatenate([none, centres[1]], axis=1)], axis=0)
         gram = lax.dot_general(left, right, NT, precision=HIGHEST, preferred_element_type=f32)
         system = gram * (1.0 / 63.0) + unit
         systems.append([system[8 * t:8 * t + 8] for t in range(9)])
@@ -293,7 +316,10 @@
 
     keep = top == (lax.rem(lane, 8) < 4)
     for i in range(BLK):
-        t = jnp.where(lane >= 64, -solved[i], 0.0)
+        t = -solved[i // 2]
+        if i % 2 == 0:
+            t = pltpu.roll(t, 64, 1)
+        t = jnp.where(lane >= 64, t, 0.0)
         t = t - jnp.sum(t, axis=1, keepdims=True) * (1.0 / 64.0)
         coef = jnp.where(
             lane >= 64,
@@ -310,8 +336,8 @@
         an_v[pl.ds(32 * m, 8, stride=4), :] = states[m][0]
         an_v[pl.ds(32 * m + 3, 8, stride=4), :] = states[m][3]
 
-    for d in range(1, NBAS):
-        g_copy(d).wait_send()
+    for step in STEPS:
+        g_copy(step).wait_send()
     for slot in range(1, NMEM):
         s_copy(0, slot, 1).wait_send()
         x_copy(0, slot, 1).wait_send()

time: 38.2 us -> 37.3 us (0.976); the launches traced: 38 us -> 36.7 us
  Pallas kernels: 37.4 us -> 36 us
    pallas_call x1, Pallas kernels: 36.6 us -> 35.2 us  [on_device(): pl.pallas_call(kernel, out_shape=(jax.ShapeDtypeStruct((128, 128), f32),...]
where the time goes in v3:
time: 37.3 us; the launch traced here: 36.7 us
  Pallas kernels  36 us (97%)
  between operations  0.64 us (2%)
    pallas_call x1, Pallas kernels, on_device(): pl.pallas_call(kernel, out_shape=(jax.ShapeDtypeStruct((128, 128), f32),...  35.2 us
    pallas_call x1, Pallas kernels, on_device(): pl.pallas_call(hand_over, out_shape=(jax.ShapeDtypeStruct((128, 128), f32...  0.78 us

profile of v3, /device:TPU:1, one launch (start us, length us, event | category | flops | bytes accessed | tf_op | source)
XLA Modules:
  0.0 36.7 jit_solution(15298510614423844516)
XLA Ops:
  0.6 35.2 %shard_map.122 = (f32[128,128]{1,0:T(8,128)S(1)}, f32[768,128]{1,0:T(8,128)S(1)}) custom-call(f32[128,128]{1,0:T(8,128)} %bitcast.35, f32[10,1024]{1,0:T(8,128)} %prm.1, f32[768,128]{1,0:T(8,128)} %bitcast.32, f32[192,128]{1,0:T(8,128)} %bitcast.33, f32[192,128]{1,0:T(8,128)} %bitcast.34, f32[4,32]{1,0:T(4,128)} %meas.1, f32[4,32]{1,0:T(4,128)} %sig.1, ...), custom_call_target="tpu_custom_call" | custom-call | tf_op jit(solution)/shard_map/pallas_call | solution.py:364
  35.9 0.8 %shard_map.123 = (f32[128,128]{1,0:T(8,128)}, f32[768,128]{1,0:T(8,128)}) custom-call(f32[128,128]{1,0:T(8,128)S(1)} %get-tuple-element.6.an, f32[768,128]{1,0:T(8,128)S(1)} %get-tuple-element.7.q), custom_call_target="tpu_custom_call" | custom-call | tf_op jit(solution)/shard_map/pallas_call | solution.py:384

commit v4 on v3

--- a/solution.py
+++ b/solution.py
@@ -17,10 +17,10 @@
 MEM = 4
 NBAS = 32
 NMEM = 16
-X_REACH = 3
-S_REACH = 4
-REACH = 4
-ORDER = ('S0', 'X3', 'S4', 'W', 'X6')
+X_SPANS = (3, 3, 2)
+S_SPANS = (4, 4)
+REACH = max(X_SPANS + S_SPANS)
+ORDER = ('S', 'X', 'S', 'X', 'W')
 LIMIT = 16 * 1024 * 1024
 
 MESH = pl.DeviceIdType.MESH
@@ -126,9 +126,6 @@
     row = lax.broadcasted_iota(jnp.int32, shape, 0)
     top = row < 4
 
-    def zmod(v):
-        return lax.rem(v + 2 * NMEM, NMEM)
-
     loads = []
     for src, dst in ((sig, sig_v), (flag, flag_v), (meas, meas_v), (draws, draws_v), (pos, pos_v),
                      (prm, prm_v), (temp, temp_v), (evap, evap_v), (init, init_v), (rain, rain_v), (adj_hbm, adj)):
@@ -138,17 +135,21 @@
 
     barrier = pltpu.get_barrier_semaphore()
 
-    me_y, me_x, me_c = me_b // 8, (me_b // 2) % 4, me_b % 2
+    me_y, me_x, me_c = lax.div(me_b, 8), lax.rem(lax.div(me_b, 2), 4), lax.rem(me_b, 2)
+
+    to_y = [lax.rem(me_y + d, 4) * 8 for d in range(4)]
+    to_x = [lax.rem(me_x + d, 4) * 2 for d in range(4)]
+    to_c = [lax.rem(me_c + d, 2) for d in range(2)]
+    to_z = [lax.rem(me_z + d, NMEM) for d in range(NMEM)]
 
     def there(step):
-        dy, dx, dc = step
-        return {"basin": ((me_y + dy) % 4 * 4 + (me_x + dx) % 4) * 2 + (me_c + dc) % 2}
+        return {"basin": to_y[step[0]] + to_x[step[1]] + to_c[step[2]]}
 
     for step in STEPS:
         pl.semaphore_signal(barrier, inc=1, device_id=there(step), device_id_type=MESH)
     for d in range(1, REACH + 1):
         for to in {d, NMEM - d}:
-            pl.semaphore_signal(barrier, inc=1, device_id={"member": zmod(me_z + to)}, device_id_type=MESH)
+            pl.semaphore_signal(barrier, inc=1, device_id={"member": to_z[to % NMEM]}, device_id_type=MESH)
 
     for cp in loads[:5]:
         cp.wait()
@@ -225,7 +226,7 @@
     def z_copy(buf, send, recv, src, slot, to):
         return pltpu.make_async_remote_copy(
             buf.at[src], buf.at[slot], send.at[slot - 1], recv.at[slot - 1],
-            device_id={"member": zmod(me_z + to)}, device_id_type=MESH)
+            device_id={"member": to_z[to % NMEM]}, device_id_type=MESH)
 
     def x_copy(src, slot, to):
         return z_copy(xz, xs_sem, xr_sem, src, slot, to)
@@ -233,19 +234,20 @@
     def s_copy(src, slot, to):
         return z_copy(sz, ss_sem, sr_sem, src, slot, to)
 
-    def spread(copy, reach, base):
+    def spread(copy, spans, stage):
+        base = sum(spans[:stage])
         if base:
             copy(0, base, 1).wait_recv()
             copy(0, NMEM - base, 1).wait_recv()
-        for d in range(min(reach, 8 - base), 0, -1):
+        for d in range(spans[stage], 0, -1):
             copy(base, base + d, d).start()
             if base + d < 8:
                 copy((NMEM - base) % NMEM, NMEM - base - d, -d).start()
 
-    def settle(copy, reach):
+    def settle(copy, spans):
+        relayed = [sum(spans[:stage]) for stage in range(1, len(spans))]
         for slot in range(1, NMEM):
-            hop = min(slot, NMEM - slot)
-            if hop % reach or hop == 8:
+            if min(slot, NMEM - slot) not in relayed:
                 copy(0, slot, 1).wait_recv()
 
     def g_copy(step):
@@ -256,7 +258,17 @@
 
     for step in STEPS:
         g_copy(step).start()
-    spread(x_copy, X_REACH, 0)
+    spread(x_copy, X_SPANS, 0)
+
+    for m in range(MEM):
+        an_v[pl.ds(32 * m, 8, stride=4), :] = states[m][0]
+        an_v[pl.ds(32 * m + 3, 8, stride=4), :] = states[m][3]
+    places = []
+    for i in range(BLK):
+        for j in range(NBR):
+            n = adj[j, me_b * BLK + i]
+            slot = (((me_y - (n >> 5)) & 3) * 8 + ((me_x - (n >> 3)) & 3) * 2 + ((me_c - (n >> 2)) & 1))
+            places.append((slot, (OBS * (j + 1) - OBS * (n & 3)) & 127))
     for step in reversed(STEPS):
         g_copy(step).wait_recv()
 
@@ -264,9 +276,7 @@
     for i in range(BLK):
         piece = tile if i == 0 else pltpu.roll(tile, 128 - OBS * i, 1)
         for j in range(NBR):
-            n = adj[j, me_b * BLK + i]
-            slot = ((me_y + 4 - n // 32) % 4 * 4 + (me_x + 4 - n // 8 % 4) % 4) * 2 + (me_c + 2 - n // 4 % 2) % 2
-            shift = lax.rem(OBS * (j + 1) + 128 - OBS * lax.rem(n, BLK), 128)
+            slot, shift = places[i * NBR + j]
             far = pltpu.roll(gath[slot], shift, 1)
             piece = jnp.where(lax.div(lane, OBS) == j + 1, far, piece)
         local.append(piece)
@@ -275,12 +285,16 @@
         sz[0, 8 * p:8 * p + 8, :] = jnp.where(top, local[2 * p], turned[2 * p + 1])
     obs_side = [jnp.where(top, t, p) for t, p in zip(turned, local)]
 
+    stage = {"S": 0, "X": 1}
     for what in ORDER:
         if what == "W":
-            settle(s_copy, S_REACH)
-        else:
-            copy, reach = (s_copy, S_REACH) if what[0] == "S" else (x_copy, X_REACH)
-            spread(copy, reach, int(what[1:]))
+            settle(s_copy, S_SPANS)
+        elif what == "S":
+            spread(s_copy, S_SPANS, stage[what])
+            stage[what] += 1
+        elif stage[what] < len(X_SPANS):
+            spread(x_copy, X_SPANS, stage[what])
+            stage[what] += 1
 
     systems = []
     big_row = lax.broadcasted_iota(jnp.int32, (72, 128), 0)
@@ -312,7 +326,12 @@
         systems.append([system[8 * t:8 * t + 8] for t in range(9)])
     solved = eliminate(systems)
 
-    settle(x_copy, X_REACH)
+    for step in STEPS:
+        g_copy(step).wait_send()
+    for slot in range(1, NMEM):
+        s_copy(0, slot, 1).wait_send()
+        x_copy(0, slot, 1).wait_send()
+    settle(x_copy, X_SPANS)
 
     keep = top == (lax.rem(lane, 8) < 4)
     for i in range(BLK):
@@ -332,15 +351,6 @@
                 coef, stored, precision=HIGHEST, preferred_element_type=f32)
             an_v[pl.ds(4 * s + 1, 4, stride=32), :] = new[0:4]
             an_v[pl.ds(4 * s + 2, 4, stride=32), :] = new[4:8]
-    for m in range(MEM):
-        an_v[pl.ds(32 * m, 8, stride=4), :] = states[m][0]
-        an_v[pl.ds(32 * m + 3, 8, stride=4), :] = states[m][3]
-
-    for step in STEPS:
-        g_copy(step).wait_send()
-    for slot in range(1, NMEM):
-        s_copy(0, slot, 1).wait_send()
-        x_copy(0, slot, 1).wait_send()
 
 
 def hand_over(an, q, an_out, q_out, sem):

time: 37.3 us -> 36.6 us (0.981); the launches traced: 36.7 us -> 36.4 us
  no operation moved by 1% of the time
where the time goes in v4:
time: 36.6 us; the launch traced here: 36.4 us
  Pallas kernels  35.7 us (98%)
  between operations  0.64 us (2%)
    pallas_call x1, Pallas kernels, on_device(): pl.pallas_call(kernel, out_shape=(jax.ShapeDtypeStruct((128, 128), f32),...  35 us
    pallas_call x1, Pallas kernels, on_device(): pl.pallas_call(hand_over, out_shape=(jax.ShapeDtypeStruct((128, 128), f32...  0.78 us

profile of v4, /device:TPU:1, one launch (start us, length us, event | category | flops | bytes accessed | tf_op | source)
XLA Modules:
  0.0 36.4 jit_solution(17945813191178161592)
XLA Ops:
  0.6 35.0 %shard_map.122 = (f32[128,128]{1,0:T(8,128)S(1)}, f32[768,128]{1,0:T(8,128)S(1)}) custom-call(f32[128,128]{1,0:T(8,128)} %bitcast.35, f32[10,1024]{1,0:T(8,128)} %prm.1, f32[768,128]{1,0:T(8,128)} %bitcast.32, f32[192,128]{1,0:T(8,128)} %bitcast.33, f32[192,128]{1,0:T(8,128)} %bitcast.34, f32[4,32]{1,0:T(4,128)} %meas.1, f32[4,32]{1,0:T(4,128)} %sig.1, ...), custom_call_target="tpu_custom_call" | custom-call | tf_op jit(solution)/shard_map/pallas_call | solution.py:374
  35.6 0.8 %shard_map.123 = (f32[128,128]{1,0:T(8,128)}, f32[768,128]{1,0:T(8,128)}) custom-call(f32[128,128]{1,0:T(8,128)S(1)} %get-tuple-element.6.an, f32[768,128]{1,0:T(8,128)S(1)} %get-tuple-element.7.q), custom_call_target="tpu_custom_call" | custom-call | tf_op jit(solution)/shard_map/pallas_call | solution.py:394

commit v5 on v4

--- a/solution.py
+++ b/solution.py
@@ -238,9 +238,11 @@
         base = sum(spans[:stage])
         if base:
             copy(0, base, 1).wait_recv()
+        for d in range(spans[stage], 0, -1):
+            copy(base, base + d, d).start()
+        if base:
             copy(0, NMEM - base, 1).wait_recv()
         for d in range(spans[stage], 0, -1):
-            copy(base, base + d, d).start()
             if base + d < 8:
                 copy((NMEM - base) % NMEM, NMEM - base - d, -d).start()
 
@@ -345,10 +347,15 @@
             jnp.where(top, pltpu.roll(t, 124, 1), t),
             jnp.where(top, pltpu.roll(t, 64, 1), pltpu.roll(t, 68, 1)))
         coef = jnp.where(keep, coef, 0.0)
+        coef_high = coef.astype(jnp.bfloat16).astype(f32)
+        factors = jnp.concatenate([coef_high, coef - coef_high], axis=0).astype(jnp.bfloat16)
         for s in (2 * i, 2 * i + 1):
             stored = xz[:, 8 * s:8 * s + 8, :].reshape(128, 128)
-            new = xz[0, 8 * s:8 * s + 8, :] + jnp.dot(
-                coef, stored, precision=HIGHEST, preferred_element_type=f32)
+            high = stored.astype(jnp.bfloat16)
+            rest = (stored - high.astype(f32)).astype(jnp.bfloat16)
+            first = jnp.dot(factors, high, preferred_element_type=f32)
+            second = jnp.dot(factors, rest, preferred_element_type=f32)
+            new = xz[0, 8 * s:8 * s + 8, :] + (first[0:8] + (first[8:16] + second[0:8]))
             an_v[pl.ds(4 * s + 1, 4, stride=32), :] = new[0:4]
             an_v[pl.ds(4 * s + 2, 4, stride=32), :] = new[4:8]
 

time: 36.6 us -> 36.3 us (level)
  no operation moved by 1% of the time
where the time goes in v5:
time: 36.3 us; the launch traced here: 36.1 us
  Pallas kernels  35.5 us (98%)
  between operations  0.64 us (2%)
    pallas_call x1, Pallas kernels, on_device(): pl.pallas_call(kernel, out_shape=(jax.ShapeDtypeStruct((128, 128), f32),...  34.7 us
    pallas_call x1, Pallas kernels, on_device(): pl.pallas_call(hand_over, out_shape=(jax.ShapeDtypeStruct((128, 128), f32...  0.78 us

profile of v5, /device:TPU:1, one launch (start us, length us, event | category | flops | bytes accessed | tf_op | source)
XLA Modules:
  0.0 36.1 jit_solution(5252664025779514869)
XLA Ops:
  0.6 34.7 %shard_map.122 = (f32[128,128]{1,0:T(8,128)S(1)}, f32[768,128]{1,0:T(8,128)S(1)}) custom-call(f32[128,128]{1,0:T(8,128)} %bitcast.35, f32[10,1024]{1,0:T(8,128)} %prm.1, f32[768,128]{1,0:T(8,128)} %bitcast.32, f32[192,128]{1,0:T(8,128)} %bitcast.33, f32[192,128]{1,0:T(8,128)} %bitcast.34, f32[4,32]{1,0:T(4,128)} %meas.1, f32[4,32]{1,0:T(4,128)} %sig.1, ...), custom_call_target="tpu_custom_call" | custom-call | tf_op jit(solution)/shard_map/pallas_call | solution.py:381
  35.3 0.8 %shard_map.123 = (f32[128,128]{1,0:T(8,128)}, f32[768,128]{1,0:T(8,128)}) custom-call(f32[128,128]{1,0:T(8,128)S(1)} %get-tuple-element.6.an, f32[768,128]{1,0:T(8,128)S(1)} %get-tuple-element.7.q), custom_call_target="tpu_custom_call" | custom-call | tf_op jit(solution)/shard_map/pallas_call | solution.py:401
